TPU v7x, 32 devices: a whole 2x2x4 slice. The times are simulated.
32 devices in a mesh: member: 16 (over z, y, x), domain: 2 (over core).
Axes of the slice: x: 2, y: 2, z: 4, core: 2. Of those that a mesh axis runs over, the one named last changes fastest.
Arguments:
- state: bfloat16 [512, 32768], P('member', 'domain'), may hold values from -6 to 6
- predicted: bfloat16 [512, 65536], P('member', 'domain'), may hold values from -6 to 6
- perturbed: bfloat16 [512, 65536], P('member', 'domain'), may hold values from -6 to 6
- obs_weight: float32 [65536], P('domain'), may hold values from 0.3 to 3
- obs_position: int32 [65536], P('domain'), may hold values from 0 to 63
- row_count: int32 [2, 32], P(None, 'member'), may hold values from 256 to 2048
- row_index: int32 [2, 32, 2048], P('domain', 'member'), may hold values from 0 to 2047, as said below
Outputs:
- updated: bfloat16 [512, 32768], P('member', 'domain')
Inputs may be any that keep to these rules, and one draw needn't show every extreme that they name: `row_index`: for each block, 2048 distinct rows of its pool; only the first row_count of them are used.
All inputs are finite; a program needn't handle non-finite values.
Results may differ from a plain program's by a relative error of at most 0.0054.
Values may be sent and summed in bfloat16 or wider, within the bound.
A program may use at most 128 MiB of HBM per device.

v0:
```python
import jax
import jax.numpy as jnp
from jax import lax
from jax.sharding import PartitionSpec as P

NS_STEPS = 5
SPAN = 2
LANES = 128


def product(left, right):
    return jnp.dot(left, right, precision=lax.Precision.HIGH)


def row_product(left, right):
    return lax.dot_general(
        left, right, (((1,), (1,)), ((), ())), preferred_element_type=jnp.float32
    )


def listed_rows(index_list, row_total, pool_rows):
    places = jnp.arange(index_list.shape[0], dtype=jnp.int32)
    live = places < row_total
    high = (index_list // LANES)[None, :] == jnp.arange(pool_rows // LANES)[:, None]
    low = (index_list % LANES)[None, :] == jnp.arange(LANES)[:, None]
    marks = row_product(
        (high & live[None, :]).astype(jnp.bfloat16), low.astype(jnp.bfloat16)
    )
    return marks.reshape(1, pool_rows)


def newton_weights(gram_sum, cross_sum):
    members = gram_sum.shape[0]
    identity = jnp.eye(members, dtype=jnp.float32)
    spread = jnp.sqrt(jnp.sum(gram_sum * gram_sum))
    start = 2.0 / (2.0 + spread)
    residual = identity - start * (identity + gram_sum)
    total = identity + residual
    for _ in range(NS_STEPS - 1):
        residual = product(residual, residual)
        total = total + product(total, residual)
    return start * product(total, cross_sum)


def per_device(state, predicted, perturbed, obs_weight, obs_position, row_count, row_index):
    pred = lax.all_to_all(predicted, "member", split_axis=1, concat_axis=0, tiled=True)
    pert = lax.all_to_all(perturbed, "member", split_axis=1, concat_axis=0, tiled=True)
    cells = lax.all_to_all(state, "member", split_axis=1, concat_axis=0, tiled=True)
    groups = lax.axis_size("member")
    group_index = lax.axis_index("member")
    tile_index = lax.axis_index("domain")
    members, pool_rows = pred.shape
    blocks = row_index.shape[1]
    block_cells = cells.shape[1] // blocks
    first_block = (tile_index * groups + group_index) * blocks
    counts = lax.dynamic_index_in_dim(row_count, tile_index, 0, keepdims=False)
    weight = lax.dynamic_slice_in_dim(obs_weight, group_index * pool_rows, pool_rows)[None, :]
    place = lax.dynamic_slice_in_dim(obs_position, group_index * pool_rows, pool_rows)[None, :]
    pred_wide = pred.astype(jnp.float32)
    pred_centred = pred_wide - jnp.mean(pred_wide, axis=0, keepdims=True)
    departure = pert.astype(jnp.float32) - pred_wide
    renewed = []
    for number in range(blocks):
        offset = (place - (first_block + number)).astype(jnp.float32) / SPAN
        marks = listed_rows(row_index[0, number], counts[number], pool_rows)
        factor = marks * (weight * (1.0 / (1.0 + offset * offset)))
        scaled = (factor * pred_centred / jnp.sqrt(members - 1.0)).astype(jnp.bfloat16)
        innovation = (factor * departure).astype(jnp.bfloat16)
        gram_sum = row_product(scaled, scaled)
        cross_sum = row_product(scaled, innovation)
        weights = (newton_weights(gram_sum, cross_sum) / jnp.sqrt(members - 1.0)).astype(
            jnp.bfloat16
        )
        values = cells[:, number * block_cells : (number + 1) * block_cells].astype(jnp.float32)
        centred = (values - jnp.mean(values, axis=0, keepdims=True)).astype(jnp.bfloat16)
        change = lax.dot_general(
            weights, centred, (((0,), (0,)), ((), ())), preferred_element_type=jnp.float32
        )
        renewed.append((values + change).astype(jnp.bfloat16))
    return lax.all_to_all(
        jnp.concatenate(renewed, axis=1), "member", split_axis=0, concat_axis=1, tiled=True
    )


def solution(mesh):
    placed = (
        P("member", "domain"),
        P("member", "domain"),
        P("member", "domain"),
        P("domain"),
        P("domain"),
        P(None, "member"),
        P("domain", "member", None),
    )
    return jax.shard_map(
        per_device, mesh=mesh, in_specs=placed, out_specs=P("member", "domain"), check_vma=False
    )
```

profile of v0, /device:TPU:0, one launch (start us, length us, event | category | flops | bytes accessed | tf_op | source)
XLA Modules:
  0.0 209.1 jit_solution(13166296687024615946)
XLA Ops:
  0.0 0.0 copy-start
  0.0 0.0 copy-start.1
  0.0 2.4 %copy.40 = bf16[4,16,8,1024]{3,2,0,1:T(8,128)(2,1)} copy(bf16[4,16,8,1024]{3,2,1,0:T(8,128)(2,1)} %bitcast.96) | data formatting | bytes 2097152 | tf_op jit(solution)/shard_map/all_to_all | solution.py:48
  2.4 8.3 %all-to-all-start = ((bf16[32,16,1024]{2,0,1:T(8,128)(2,1)}), bf16[32,16,1024]{2,0,1:T(8,128)(2,1)S(1)}, u32[]{:S(2)}, u32[]{:S(2)}) async-start(bf16[32,16,1024]{2,0,1:T(8,128)(2,1)} %bitcast.82), calls=%async_computation | async-start | bytes 2097152 | tf_op jit(solution)/shard_map/all_to_all | solution.py:48
  10.8 0.0 copy-done.1
  10.8 1.5 copy.39
  12.3 22.9 %all-to-all-done = bf16[32,16,1024]{2,0,1:T(8,128)(2,1)S(1)} async-done(((bf16[32,16,1024]{2,0,1:T(8,128)(2,1)}), bf16[32,16,1024]{2,0,1:T(8,128)(2,1)S(1)}, u32[]{:S(2)}, u32[]{:S(2)}) %all-to-all-start) | async-done | bytes 1048608 | tf_op jit(solution)/shard_map/all_to_all | solution.py:48
  35.2 5.9 %all-to-all-start.1 = ((bf16[32,16,2048]{2,0,1:T(8,128)(2,1)}), bf16[32,16,2048]{2,0,1:T(8,128)(2,1)S(1)}, u32[]{:S(2)}, u32[]{:S(2)}) async-start(bf16[32,16,2048]{2,0,1:T(8,128)(2,1)} %bitcast.84), calls=%async_computation.1 | async-start | bytes 4194304 | tf_op jit(solution)/shard_map/all_to_all | solution.py:46
  41.1 3.2 %copy.38 = bf16[4,16,8,2048]{3,2,0,1:T(8,128)(2,1)} copy(bf16[4,16,8,2048]{3,2,1,0:T(8,128)(2,1)} %bitcast.89) | data formatting | bytes 4194304 | tf_op jit(solution)/shard_map/all_to_all | solution.py:47
  44.2 38.7 %all-to-all-done.1 = bf16[32,16,2048]{2,0,1:T(8,128)(2,1)S(1)} async-done(((bf16[32,16,2048]{2,0,1:T(8,128)(2,1)}), bf16[32,16,2048]{2,0,1:T(8,128)(2,1)S(1)}, u32[]{:S(2)}, u32[]{:S(2)}) %all-to-all-start.1) | async-done | bytes 2097184 | tf_op jit(solution)/shard_map/all_to_all | solution.py:46
  82.9 10.0 %all-to-all-start.2 = ((bf16[32,16,2048]{2,0,1:T(8,128)(2,1)}), bf16[32,16,2048]{2,0,1:T(8,128)(2,1)}, u32[]{:S(2)}, u32[]{:S(2)}) async-start(bf16[32,16,2048]{2,0,1:T(8,128)(2,1)} %bitcast.83), calls=%async_computation.2 | async-start | bytes 4194304 | tf_op jit(solution)/shard_map/all_to_all | solution.py:47
  92.9 0.0 copy-done
  92.9 0.6 fusion.44
  93.5 0.6 iota_compare_fusion.9
  94.0 0.7 iota_compare_fusion.10
  94.7 0.0 copy-done.9
  94.8 1.0 fusion.13
  95.8 1.0 fusion.12
  96.8 1.1 fusion.42
  97.9 1.3 copy.29
  99.1 1.3 copy.30
  100.4 0.1 convert_reduce_fusion.2
  100.5 0.1 convert_reduce_fusion.1
  100.7 0.4 convert_reduce_fusion
  101.1 34.4 %all-to-all-done.2 = bf16[32,16,2048]{2,0,1:T(8,128)(2,1)} async-done(((bf16[32,16,2048]{2,0,1:T(8,128)(2,1)}), bf16[32,16,2048]{2,0,1:T(8,128)(2,1)}, u32[]{:S(2)}, u32[]{:S(2)}) %all-to-all-start.2) | async-done | bytes 2097184 | tf_op jit(solution)/shard_map/all_to_all | solution.py:47
  135.5 5.2 %multiply_convert_fusion.1 = (bf16[32,16,2048]{2,0,1:T(8,128)(2,1)}, bf16[32,16,2048]{2,0,1:T(8,128)(2,1)}, bf16[32,16,2048]{2,0,1:T(8,128)(2,1)}, bf16[32,16,2048]{2,0,1:T(8,128)(2,1)S(1)}) fusion(bf16[32,16,2048]{2,0,1:T(8,128)(2,1)S(1)} %all-to-all-done.1, bf16[32,16,2048]{2,0,1:T(8,128)(2,1)} %all-to-all-done.2, f32[2048]{0:T(1024)S(1)} %fusion.13, ...), kind=kLoop, calls=%fused_computation.10 | loop fusion | flops 14680064 | bytes 12607488 | tf_op jit(solution)/shard_map/convert_element_type | solution.py:68
  140.8 2.0 multiply_reduce_fusion.1
  142.8 0.0 copy-done.6
  143.5 1.1 fusion.18
  144.6 2.0 convolution_add_fusion.7
  146.6 1.0 fusion.45
  147.7 0.5 copy-done.3
  148.2 2.1 multiply_reduce_fusion
  151.1 1.1 fusion.19
  152.2 1.1 convolution_add_fusion.3
  153.3 1.0 fusion.49
  154.3 0.0 copy-start.8
  154.3 1.0 fusion.46
  155.4 0.2 copy-done.8
  155.5 1.0 convolution_add_fusion.6
  156.6 0.0 copy-start.7
  156.6 1.0 fusion.47
  157.6 0.0 copy-start.5
  157.7 1.3 convolution_add_fusion.5
  159.0 0.0 copy-done.7
  159.0 0.4 copy-done.5
  159.4 1.3 fusion.48
  160.7 0.3 copy-done.2
  161.0 0.6 copy-done.4
  161.6 1.3 fusion.52
  162.9 1.0 fusion.50
  163.9 1.1 convolution_add_fusion.2
  165.0 1.0 fusion.51
  166.1 1.0 convolution_add_fusion.1
  167.1 1.1 convolution_add_fusion.4
  168.2 1.0 fusion.10
  169.3 0.5 fusion.8
  169.8 1.0 convolution_add_fusion
  170.8 1.0 fusion.11
  171.9 0.5 fusion.9
  172.4 0.1 pad_maximum_fusion
  172.4 0.5 copy.27
  173.0 35.1 %all_to_all.64 = bf16[16,32,1024]{2,1,0:T(8,128)(2,1)S(1)} all-to-all(bf16[16,32,1024]{2,1,0:T(8,128)(2,1)S(1)} %bitcast.86), channel_id=1, replica_groups=mesh['member'=16,'domain'=2] {'member'}, dimensions={0} | all-to-all | bytes 2097152 | tf_op jit(solution)/shard_map/all_to_all | solution.py:80
  208.1 1.1 copy.34
  (12 shorter events, 0.1 us)
Async XLA Ops:
  0.0 92.9 %copy-start = (s32[2,2]{1,0:T(2,128)S(1)}, s32[2,2]{1,0:T(2,128)}, u32[]{:S(2)}) copy-start(s32[2,2]{1,0:T(2,128)} %param.12) | copy-start | bytes 52
  0.0 10.8 %copy-start.1 = (bf16[32,32768]{1,0:T(8,128)(2,1)S(1)}, bf16[32,32768]{1,0:T(8,128)(2,1)}, u32[]{:S(2)}) copy-start(bf16[32,32768]{1,0:T(8,128)(2,1)} %param.8) | copy-start | bytes 6291460
  2.4 32.7 %all-to-all-start = ((bf16[32,16,1024]{2,0,1:T(8,128)(2,1)}), bf16[32,16,1024]{2,0,1:T(8,128)(2,1)S(1)}, u32[]{:S(2)}, u32[]{:S(2)}) async-start(bf16[32,16,1024]{2,0,1:T(8,128)(2,1)} %bitcast.82), calls=%async_computation | async-start | bytes 2097152 | tf_op jit(solution)/shard_map/all_to_all | solution.py:48
  35.2 47.7 %all-to-all-start.1 = ((bf16[32,16,2048]{2,0,1:T(8,128)(2,1)}), bf16[32,16,2048]{2,0,1:T(8,128)(2,1)S(1)}, u32[]{:S(2)}, u32[]{:S(2)}) async-start(bf16[32,16,2048]{2,0,1:T(8,128)(2,1)} %bitcast.84), calls=%async_computation.1 | async-start | bytes 4194304 | tf_op jit(solution)/shard_map/all_to_all | solution.py:46
  82.9 11.8 %copy-start.9 = (s32[1,2,2048]{2,1,0:T(2,128)S(1)}, s32[1,2,2048]{2,1,0:T(2,128)}, u32[]{:S(2)}) copy-start(s32[1,2,2048]{2,1,0:T(2,128)} %param.13) | copy-start | bytes 49156
  82.9 52.6 %all-to-all-start.2 = ((bf16[32,16,2048]{2,0,1:T(8,128)(2,1)}), bf16[32,16,2048]{2,0,1:T(8,128)(2,1)}, u32[]{:S(2)}, u32[]{:S(2)}) async-start(bf16[32,16,2048]{2,0,1:T(8,128)(2,1)} %bitcast.83), calls=%async_computation.2 | async-start | bytes 4194304 | tf_op jit(solution)/shard_map/all_to_all | solution.py:47
  140.8 2.0 copy-start.6
  146.6 1.6 copy-start.3
  154.3 1.2 copy-start.8
  156.6 2.4 %copy-start.7 = (bf16[32,16,2048]{2,0,1:T(8,128)(2,1)S(1)}, bf16[32,16,2048]{2,0,1:T(8,128)(2,1)}, u32[]{:S(2)}) copy-start(bf16[32,16,2048]{2,0,1:T(8,128)(2,1)} %copy-done.6) | copy-start | bytes 6291460
  157.6 1.7 copy-start.5
  159.4 1.6 copy-start.2
  159.4 2.2 %copy-start.4 = (bf16[32,16,2048]{2,0,1:T(8,128)(2,1)S(1)}, bf16[32,16,2048]{2,0,1:T(8,128)(2,1)}, u32[]{:S(2)}) copy-start(bf16[32,16,2048]{2,0,1:T(8,128)(2,1)} %get-tuple-element.7) | copy-start | bytes 6291460
where the time goes:
time: 210 us; the launch traced here: 209 us
  waiting for transfers between devices  96 us (46%)
  blocking collectives  35.1 us (17%)
  matrix products  29.9 us (14%)
  starting transfers between devices  24.2 us (12%)
  local copies, waits for them, and re-layouts  14.9 us (7%)
  other arithmetic  7.25 us (3%)
    all_to_all x1, waiting for transfers between devices, per_device(): lax.all_to_all(predicted, 'member', split_axis=1, concat_axis=0, tiled=True)  38.7 us
    all_to_all x1, blocking collectives, per_device(): lax.all_to_all(jnp.concatenate(renewed, axis=1), 'member', split_axis=0,...  35.1 us
    all_to_all x1, waiting for transfers between devices, per_device(): lax.all_to_all(perturbed, 'member', split_axis=1, concat_axis=0, tiled=True)  34.4 us
    all_to_all x1, waiting for transfers between devices, per_device(): lax.all_to_all(state, 'member', split_axis=1, concat_axis=0, tiled=True)  22.9 us
    dot_general x18, matrix products, product(): return jnp.dot(left, right, precision=lax.Precision.HIGH)  20.2 us
    all_to_all x1, starting transfers between devices, per_device(): lax.all_to_all(perturbed, 'member', split_axis=1, concat_axis=0, tiled=True)  9.95 us
    dot_general x6, matrix products, row_product(): lax.dot_general(left, right, (((1,), (1,)), ((), ())), preferred_element_...  8.69 us
    all_to_all x1, starting transfers between devices, per_device(): lax.all_to_all(state, 'member', split_axis=1, concat_axis=0, tiled=True)  8.34 us
  transfers between devices with their start and end apart: 3, of which 3 were waited for; matrix products, arithmetic and copies ran while one was open for 6% of the time, Pallas kernels for 0%

commit v1 on v0

v1 whole, which is shorter than its diff:
```python
import functools
import math

import jax
import jax.numpy as jnp
from jax import lax
from jax.experimental import pallas as pl
from jax.experimental.pallas import tpu as pltpu
from jax.sharding import PartitionSpec as P

NS_STEPS = 5
SPAN = 2
LANES = 128
CHUNK = 512
F32 = jnp.float32
BF16 = jnp.bfloat16


def row_product(left, right):
    return lax.dot_general(left, right, (((1,), (1,)), ((), ())), preferred_element_type=F32)


def split(value):
    high = value.astype(BF16)
    return high, (value - high.astype(F32)).astype(BF16)


def product(left, right):
    (left_high, left_low), (right_high, right_low) = left, right
    dot = functools.partial(jnp.dot, preferred_element_type=F32)
    return dot(left_high, right_high) + (dot(left_high, right_low) + dot(left_low, right_high))


def peer_order(groups):
    return sorted(range(1, groups), reverse=True)


def kernel(
    groups,
    state,
    predicted,
    perturbed,
    weight_pools,
    place_pools,
    row_count,
    row_index,
    updated,
    pred,
    pert,
    cells,
    renewed,
    weight,
    place,
    factor,
    scaled,
    gram,
    cross,
    residual_high,
    residual_low,
    total,
    inverse_high,
    inverse_low,
    gain,
    send_sem,
    recv_sem,
    own_sem,
    side_sem,
):
    me = lax.axis_index("member")
    tile = lax.axis_index("domain")
    rows_here = pred.shape[1]
    pool_rows = pred.shape[2]
    members = groups * rows_here
    blocks = row_index.shape[1]
    block_cells = cells.shape[3]
    shrink = 1.0 / math.sqrt(members - 1.0)
    peers = peer_order(groups)

    def pool_columns(group):
        return pl.ds(pl.multiple_of(group * pool_rows, pool_rows), pool_rows)

    def cell_columns(group, number):
        return pl.ds(
            pl.multiple_of((group * blocks + number) * block_cells, block_cells), block_cells
        )

    def sources(group):
        return [predicted.at[:, pool_columns(group)], perturbed.at[:, pool_columns(group)]] + [
            state.at[:, cell_columns(group, number)] for number in range(blocks)
        ]

    slots = [pred.at[me], pert.at[me]] + [cells.at[number, me] for number in range(blocks)]
    kinds = len(slots)

    side_copies = [
        pltpu.make_async_copy(weight_pools.at[me], weight, side_sem.at[0]),
        pltpu.make_async_copy(place_pools.at[me], place, side_sem.at[1]),
    ]
    own_copies = [
        pltpu.make_async_copy(source, slot, own_sem.at[kind])
        for kind, (source, slot) in enumerate(zip(sources(me), slots))
    ]
    for copy in side_copies + own_copies:
        copy.start()

    barrier = pltpu.get_barrier_semaphore()
    for step in peers:
        pl.semaphore_signal(
            barrier,
            inc=1,
            device_id=(jnp.bitwise_xor(me, step), tile),
            device_id_type=pl.DeviceIdType.MESH,
        )
    pl.semaphore_wait(barrier, groups - 1)

    def remote(source, target, kind, step):
        return pltpu.make_async_remote_copy(
            src_ref=source,
            dst_ref=target,
            send_sem=send_sem.at[kind, step],
            recv_sem=recv_sem.at[kind, step],
            device_id=(jnp.bitwise_xor(me, step), tile),
            device_id_type=pl.DeviceIdType.MESH,
        )

    incoming = [
        [
            remote(sources(jnp.bitwise_xor(me, step))[kind], slots[kind], kind, step)
            for step in peers
        ]
        for kind in range(kinds)
    ]
    for copies in incoming:
        for copy in copies:
            copy.start()

    def arrived(kind):
        own_copies[kind].wait()
        for copy in incoming[kind]:
            copy.wait_recv()

    for copy in side_copies:
        copy.wait()
    for number in range(blocks):
        first_block = (tile * groups + me) * blocks
        picked = row_index[0, number : number + 1, :]
        length = picked.shape[1]
        live = lax.broadcasted_iota(jnp.int32, (1, length), 1) < row_count[tile, number]
        high = lax.broadcasted_iota(jnp.int32, (pool_rows // LANES, length), 0)
        low = lax.broadcasted_iota(jnp.int32, (LANES, length), 0)
        in_high = jnp.where((high == picked // LANES) & live, 1.0, 0.0).astype(BF16)
        in_low = jnp.where(low == picked % LANES, 1.0, 0.0).astype(BF16)
        marks = row_product(in_high, in_low)
        marks = jnp.concatenate(
            [marks[part : part + 1, :] for part in range(pool_rows // LANES)], axis=1
        )
        offset = (place[...] - (first_block + number)).astype(F32) / SPAN
        factor[number, :, :] = marks * (weight[...] * (1.0 / (1.0 + offset * offset)))

    arrived(0)

    def clear(number):
        gram[number] = jnp.zeros((members, members), F32)
        cross[number] = jnp.zeros((members, members), F32)

    for number in range(blocks):
        clear(number)

    def chunk_columns(chunk):
        return pl.ds(pl.multiple_of(chunk * CHUNK, CHUNK), CHUNK)

    def add_gram(chunk, carry):
        columns = chunk_columns(chunk)
        values = pred[:, :, columns].reshape(members, CHUNK).astype(F32)
        values = values - jnp.sum(values, axis=0, keepdims=True) * (1.0 / members)
        for number in range(blocks):
            rows = (factor[number, :, columns] * values * shrink).astype(BF16)
            scaled[number, :, columns] = rows
            gram[number] += row_product(rows, rows)
        return carry

    lax.fori_loop(0, pool_rows // CHUNK, add_gram, 0)

    def invert(number, carry):
        gram_sum = gram[number]
        squares = jnp.sum(gram_sum * gram_sum, axis=0, keepdims=True)
        spread = jnp.sqrt(jnp.sum(squares, axis=1, keepdims=True))
        start = 2.0 / (2.0 + spread)
        row = lax.broadcasted_iota(jnp.int32, (members, members), 0)
        column = lax.broadcasted_iota(jnp.int32, (members, members), 1)
        identity = jnp.where(row == column, 1.0, 0.0)
        residual = identity - start * (identity + gram_sum)
        total[...] = identity + residual
        residual_high[...], residual_low[...] = split(residual)

        def double(step, carry):
            held = (residual_high[...], residual_low[...])
            held = split(product(held, held))
            residual_high[...], residual_low[...] = held
            total[...] += product(split(total[...]), held)
            return carry

        lax.fori_loop(0, NS_STEPS - 1, double, 0)
        inverse_high[number], inverse_low[number] = split(start * total[...])
        return carry

    lax.fori_loop(0, blocks, invert, 0)

    arrived(1)

    def add_cross(chunk, carry):
        columns = chunk_columns(chunk)
        values = pert[:, :, columns].reshape(members, CHUNK).astype(F32)
        values = values - pred[:, :, columns].reshape(members, CHUNK).astype(F32)
        for number in range(blocks):
            rows = (factor[number, :, columns] * values).astype(BF16)
            cross[number] += row_product(rows, scaled[number, :, columns])
        return carry

    lax.fori_loop(0, pool_rows // CHUNK, add_cross, 0)

    def weigh(number, carry):
        weights = product(split(cross[number]), (inverse_high[number], inverse_low[number]))
        gain[number] = (weights * shrink).astype(BF16)
        return carry

    lax.fori_loop(0, blocks, weigh, 0)

    outgoing = []
    own_out = []
    for number in range(blocks):
        arrived(2 + number)
        values = cells[number].reshape(members, block_cells).astype(F32)
        centred = (values - jnp.sum(values, axis=0, keepdims=True) * (1.0 / members)).astype(BF16)
        change = jnp.dot(gain[number], centred, preferred_element_type=F32)
        renewed[number] = (values + change).astype(BF16).reshape(groups, rows_here, block_cells)
        target = updated.at[:, cell_columns(me, number)]
        for step in peers:
            copy = remote(
                renewed.at[number, jnp.bitwise_xor(me, step)], target, kinds + number, step
            )
            copy.start()
            outgoing.append(copy)
        copy = pltpu.make_async_copy(renewed.at[number, me], target, own_sem.at[kinds + number])
        copy.start()
        own_out.append(copy)

    for copies in incoming:
        for copy in copies:
            copy.wait_send()
    for copy in own_out:
        copy.wait()
    for copy in outgoing:
        copy.wait()


def per_device(groups, state, predicted, perturbed, obs_weight, obs_position, row_count, row_index):
    rows_here, cells_all = state.shape
    pool_rows = predicted.shape[1] // groups
    members = groups * rows_here
    blocks = row_index.shape[1]
    block_cells = cells_all // groups // blocks
    kinds = 2 + 2 * blocks
    anywhere = pl.BlockSpec(memory_space=pl.ANY)
    square = (blocks, members, members)
    return pl.pallas_call(
        functools.partial(kernel, groups),
        out_shape=jax.ShapeDtypeStruct(state.shape, state.dtype),
        in_specs=[anywhere] * 5
        + [pl.BlockSpec(memory_space=pltpu.SMEM), pl.BlockSpec(memory_space=pltpu.VMEM)],
        out_specs=anywhere,
        scratch_shapes=[
            pltpu.VMEM((groups, rows_here, pool_rows), BF16),
            pltpu.VMEM((groups, rows_here, pool_rows), BF16),
            pltpu.VMEM((blocks, groups, rows_here, block_cells), BF16),
            pltpu.VMEM((blocks, groups, rows_here, block_cells), BF16),
            pltpu.VMEM((1, pool_rows), F32),
            pltpu.VMEM((1, pool_rows), jnp.int32),
            pltpu.VMEM((blocks, 1, pool_rows), F32),
            pltpu.VMEM((blocks, members, pool_rows), BF16),
            pltpu.VMEM(square, F32),
            pltpu.VMEM(square, F32),
            pltpu.VMEM((members, members), BF16),
            pltpu.VMEM((members, members), BF16),
            pltpu.VMEM((members, members), F32),
            pltpu.VMEM(square, BF16),
            pltpu.VMEM(square, BF16),
            pltpu.VMEM(square, BF16),
            pltpu.SemaphoreType.DMA((kinds, groups)),
            pltpu.SemaphoreType.DMA((kinds, groups)),
            pltpu.SemaphoreType.DMA((kinds,)),
            pltpu.SemaphoreType.DMA((2,)),
        ],
        compiler_params=pltpu.CompilerParams(
            collective_id=0, has_side_effects=True, vmem_limit_bytes=56 * 2**20
        ),
    )(
        state,
        predicted,
        perturbed,
        obs_weight.reshape(groups, 1, pool_rows),
        obs_position.reshape(groups, 1, pool_rows),
        row_count,
        row_index,
    )


def solution(mesh):
    placed = (
        P("member", "domain"),
        P("member", "domain"),
        P("member", "domain"),
        P("domain"),
        P("domain"),
        P(None, "member"),
        P("domain", "member", None),
    )
    return jax.shard_map(
        functools.partial(per_device, mesh.shape["member"]),
        mesh=mesh,
        in_specs=placed,
        out_specs=P("member", "domain"),
        check_vma=False,
    )
```

time: 210 us -> 155 us (0.74)
  Pallas kernels: 0 us -> 152 us
  waiting for transfers between devices: 96 us -> 0 us
  blocking collectives: 35.1 us -> 0 us
  matrix products: 29.9 us -> 0 us
  starting transfers between devices: 24.2 us -> 0 us
  local copies, waits for them, and re-layouts: 14.9 us -> 2.26 us
  other arithmetic: 7.25 us -> 0 us
    pallas_call x0 -> x1, Pallas kernels: none -> 152 us  [per_device(): pl.pallas_call(functools.partial(kernel, groups), out_shape=jax.ShapeDtyp...]
    all_to_all x3 -> x0, waiting for transfers between devices: 96 us -> none  [the longest x1 38.7 us: per_device(): lax.all_to_all(predicted, 'member', split_axis=1, concat_axis=0, tiled=True)]
    all_to_all x1 -> x0, blocking collectives: 35.1 us -> none  [per_device(): lax.all_to_all(jnp.concatenate(renewed, axis=1), 'member', split_axis=0,...]
    dot_general x26 -> x0, matrix products: 29.9 us -> none  [the longest x18 20.2 us: product(): return jnp.dot(left, right, precision=lax.Precision.HIGH)]
    all_to_all x3 -> x0, starting transfers between devices: 24.2 us -> none  [the longest x1 9.95 us: per_device(): lax.all_to_all(perturbed, 'member', split_axis=1, concat_axis=0, tiled=True)]
    all_to_all x4 -> x0, local copies, waits for them, and re-layouts: 8.13 us -> none  [the longest x1 3.16 us: per_device(): lax.all_to_all(perturbed, 'member', split_axis=1, concat_axis=0, tiled=True)]
    convert_element_type x1 -> x0, other arithmetic: 5.25 us -> none  [per_device(): innovation = (factor * departure).astype(jnp.bfloat16)]
    unnamed x22 -> x1, local copies, waits for them, and re-layouts: 4.58 us -> 2.26 us
  transfers between devices with their start and end apart: 3 -> 0, of which waited for: 3 -> 0; matrix products, arithmetic and copies ran while one was open for 6% -> 0% of each run, Pallas kernels for 0% -> 0%
where the time goes in v1:
time: 155 us; the launch traced here: 154 us
  Pallas kernels  152 us (98%)
  local copies, waits for them, and re-layouts  2.26 us (1%)
    pallas_call x1, Pallas kernels, per_device(): pl.pallas_call(functools.partial(kernel, groups), out_shape=jax.ShapeDtyp...  152 us

profile of v1, /device:TPU:0, one launch (start us, length us, event | category | flops | bytes accessed | tf_op | source)
XLA Modules:
  0.0 154.3 jit_solution(17102256786205891764)
XLA Ops:
  0.0 152.0 %shard_map.73 = bf16[32,16384]{1,0:T(8,128)(2,1)} custom-call(bf16[32,16384]{1,0:T(8,128)(2,1)} %state.1, bf16[32,32768]{1,0:T(8,128)(2,1)} %predicted.1, bf16[32,32768]{1,0:T(8,128)(2,1)} %perturbed.1, f32[16,1,2048]{2,1,0:T(1,128)} %bitcast.2, s32[16,1,2048]{2,1,0:T(1,128)} %bitcast.3, s32[2,2]{1,0:T(2,128)} %row_count.1, s32[1,2,2048]{2,1,0:T(2,128)} %row_index.1), custom_call_target="tpu_custom_call" | custom-call | tf_op jit(solution)/shard_map/pallas_call | solution.py:266
  152.1 2.3 %copy.9 = bf16[32,16384]{1,0:T(8,128)(2,1)} copy(bf16[32,16384]{1,0:T(8,128)(2,1)} %shard_map.73) | data formatting | bytes 2097152

commit v2 on v1

--- a/solution.py
+++ b/solution.py
@@ -31,8 +31,10 @@
     return dot(left_high, right_high) + (dot(left_high, right_low) + dot(left_low, right_high))
 
 
-def peer_order(groups):
-    return sorted(range(1, groups), reverse=True)
+def send_orders(groups):
+    near_first = list(range(1, groups))
+    far_first = near_first[groups // 2 - 1 :] + near_first[: groups // 2 - 1]
+    return list(zip(near_first, far_first))
 
 
 def kernel(
@@ -45,6 +47,8 @@
     row_count,
     row_index,
     updated,
+    counts,
+    lists,
     pred,
     pert,
     cells,
@@ -74,7 +78,8 @@
     blocks = row_index.shape[1]
     block_cells = cells.shape[3]
     shrink = 1.0 / math.sqrt(members - 1.0)
-    peers = peer_order(groups)
+    peers = list(range(1, groups))
+    orders = send_orders(groups)
 
     def pool_columns(group):
         return pl.ds(pl.multiple_of(group * pool_rows, pool_rows), pool_rows)
@@ -95,14 +100,13 @@
     side_copies = [
         pltpu.make_async_copy(weight_pools.at[me], weight, side_sem.at[0]),
         pltpu.make_async_copy(place_pools.at[me], place, side_sem.at[1]),
+        pltpu.make_async_copy(row_count, counts, side_sem.at[2]),
+        pltpu.make_async_copy(row_index, lists, side_sem.at[3]),
     ]
     own_copies = [
         pltpu.make_async_copy(source, slot, own_sem.at[kind])
         for kind, (source, slot) in enumerate(zip(sources(me), slots))
     ]
-    for copy in side_copies + own_copies:
-        copy.start()
-
     barrier = pltpu.get_barrier_semaphore()
     for step in peers:
         pl.semaphore_signal(
@@ -111,6 +115,8 @@
             device_id=(jnp.bitwise_xor(me, step), tile),
             device_id_type=pl.DeviceIdType.MESH,
         )
+    for copy in side_copies + own_copies:
+        copy.start()
     pl.semaphore_wait(barrier, groups - 1)
 
     def remote(source, target, kind, step):
@@ -130,9 +136,13 @@
         ]
         for kind in range(kinds)
     ]
-    for copies in incoming:
-        for copy in copies:
-            copy.start()
+    def chosen(order):
+        return order[0] + (order[1] - order[0]) * (tile % 2)
+
+    for kind in range(kinds):
+        for order in orders:
+            step = chosen(order)
+            remote(sources(jnp.bitwise_xor(me, step))[kind], slots[kind], kind, step).start()
 
     def arrived(kind):
         own_copies[kind].wait()
@@ -143,9 +153,9 @@
         copy.wait()
     for number in range(blocks):
         first_block = (tile * groups + me) * blocks
-        picked = row_index[0, number : number + 1, :]
+        picked = lists[0, number : number + 1, :]
         length = picked.shape[1]
-        live = lax.broadcasted_iota(jnp.int32, (1, length), 1) < row_count[tile, number]
+        live = lax.broadcasted_iota(jnp.int32, (1, length), 1) < counts[tile, number]
         high = lax.broadcasted_iota(jnp.int32, (pool_rows // LANES, length), 0)
         low = lax.broadcasted_iota(jnp.int32, (LANES, length), 0)
         in_high = jnp.where((high == picked // LANES) & live, 1.0, 0.0).astype(BF16)
@@ -235,12 +245,15 @@
         change = jnp.dot(gain[number], centred, preferred_element_type=F32)
         renewed[number] = (values + change).astype(BF16).reshape(groups, rows_here, block_cells)
         target = updated.at[:, cell_columns(me, number)]
-        for step in peers:
-            copy = remote(
+
+        def give(step, number=number, target=target):
+            return remote(
                 renewed.at[number, jnp.bitwise_xor(me, step)], target, kinds + number, step
             )
-            copy.start()
-            outgoing.append(copy)
+
+        for order in orders:
+            give(chosen(order)).start()
+        outgoing += [give(step) for step in peers]
         copy = pltpu.make_async_copy(renewed.at[number, me], target, own_sem.at[kinds + number])
         copy.start()
         own_out.append(copy)
@@ -266,10 +279,11 @@
     return pl.pallas_call(
         functools.partial(kernel, groups),
         out_shape=jax.ShapeDtypeStruct(state.shape, state.dtype),
-        in_specs=[anywhere] * 5
-        + [pl.BlockSpec(memory_space=pltpu.SMEM), pl.BlockSpec(memory_space=pltpu.VMEM)],
+        in_specs=[anywhere] * 7,
         out_specs=anywhere,
         scratch_shapes=[
+            pltpu.SMEM(row_count.shape, jnp.int32),
+            pltpu.VMEM(row_index.shape, jnp.int32),
             pltpu.VMEM((groups, rows_here, pool_rows), BF16),
             pltpu.VMEM((groups, rows_here, pool_rows), BF16),
             pltpu.VMEM((blocks, groups, rows_here, block_cells), BF16),
@@ -289,7 +303,7 @@
             pltpu.SemaphoreType.DMA((kinds, groups)),
             pltpu.SemaphoreType.DMA((kinds, groups)),
             pltpu.SemaphoreType.DMA((kinds,)),
-            pltpu.SemaphoreType.DMA((2,)),
+            pltpu.SemaphoreType.DMA((4,)),
         ],
         compiler_params=pltpu.CompilerParams(
             collective_id=0, has_side_effects=True, vmem_limit_bytes=56 * 2**20

time: 155 us -> 147 us (0.948)
  Pallas kernels: 152 us -> 144 us
    pallas_call x1, Pallas kernels: 152 us -> 144 us  [per_device(): pl.pallas_call(functools.partial(kernel, groups), out_shape=jax.ShapeDtyp...]
where the time goes in v2:
time: 147 us; the launch traced here: 146 us
  Pallas kernels  144 us (98%)
  local copies, waits for them, and re-layouts  2.26 us (2%)
    pallas_call x1, Pallas kernels, per_device(): pl.pallas_call(functools.partial(kernel, groups), out_shape=jax.ShapeDtyp...  144 us

profile of v2, /device:TPU:0, one launch (start us, length us, event | category | flops | bytes accessed | tf_op | source)
XLA Modules:
  0.0 146.4 jit_solution(2863520196813523137)
XLA Ops:
  0.0 144.2 %shard_map.73 = bf16[32,16384]{1,0:T(8,128)(2,1)} custom-call(bf16[32,16384]{1,0:T(8,128)(2,1)} %state.1, bf16[32,32768]{1,0:T(8,128)(2,1)} %predicted.1, bf16[32,32768]{1,0:T(8,128)(2,1)} %perturbed.1, f32[16,1,2048]{2,1,0:T(1,128)} %bitcast.2, s32[16,1,2048]{2,1,0:T(1,128)} %bitcast.3, s32[2,2]{1,0:T(2,128)} %row_count.1, s32[1,2,2048]{2,1,0:T(2,128)} %row_index.1), custom_call_target="tpu_custom_call" | custom-call | tf_op jit(solution)/shard_map/pallas_call | solution.py:279
  144.2 2.3 %copy.9 = bf16[32,16384]{1,0:T(8,128)(2,1)} copy(bf16[32,16384]{1,0:T(8,128)(2,1)} %shard_map.73) | data formatting | bytes 2097152

commit v3 on v2

--- a/solution.py
+++ b/solution.py
@@ -31,10 +31,15 @@
     return dot(left_high, right_high) + (dot(left_high, right_low) + dot(left_low, right_high))
 
 
-def send_orders(groups):
-    near_first = list(range(1, groups))
-    far_first = near_first[groups // 2 - 1 :] + near_first[: groups // 2 - 1]
+def send_orders(groups, done=()):
+    near_first = [step for step in range(1, groups) if step not in done]
+    far_first = [step for step in near_first if step >= groups // 2]
+    far_first += [step for step in near_first if step < groups // 2]
     return list(zip(near_first, far_first))
+
+
+def doublings(groups):
+    return [1 << bit for bit in range(groups.bit_length() - 1)]
 
 
 def kernel(
@@ -69,6 +74,7 @@
     recv_sem,
     own_sem,
     side_sem,
+    meet_sem,
 ):
     me = lax.axis_index("member")
     tile = lax.axis_index("domain")
@@ -108,16 +114,21 @@
         for kind, (source, slot) in enumerate(zip(sources(me), slots))
     ]
     barrier = pltpu.get_barrier_semaphore()
-    for step in peers:
+    partners = doublings(groups)[::-1]
+
+    def greet(semaphore, step):
         pl.semaphore_signal(
-            barrier,
+            semaphore,
             inc=1,
             device_id=(jnp.bitwise_xor(me, step), tile),
             device_id_type=pl.DeviceIdType.MESH,
         )
+
+    for step in partners:
+        greet(barrier, step)
     for copy in side_copies + own_copies:
         copy.start()
-    pl.semaphore_wait(barrier, groups - 1)
+    pl.semaphore_wait(barrier, len(partners))
 
     def remote(source, target, kind, step):
         return pltpu.make_async_remote_copy(
@@ -139,10 +150,19 @@
     def chosen(order):
         return order[0] + (order[1] - order[0]) * (tile % 2)
 
-    for kind in range(kinds):
+    def send(kind, step):
+        remote(sources(jnp.bitwise_xor(me, step))[kind], slots[kind], kind, step).start()
+
+    for step in partners:
+        send(0, step)
+    for number, step in enumerate(partners):
+        greet(meet_sem.at[number], step)
+        pl.semaphore_wait(meet_sem.at[number], 1)
+    for order in send_orders(groups, partners):
+        send(0, chosen(order))
+    for kind in range(1, kinds):
         for order in orders:
-            step = chosen(order)
-            remote(sources(jnp.bitwise_xor(me, step))[kind], slots[kind], kind, step).start()
+            send(kind, chosen(order))
 
     def arrived(kind):
         own_copies[kind].wait()
@@ -304,6 +324,7 @@
             pltpu.SemaphoreType.DMA((kinds, groups)),
             pltpu.SemaphoreType.DMA((kinds,)),
             pltpu.SemaphoreType.DMA((4,)),
+            pltpu.SemaphoreType.REGULAR((len(doublings(groups)),)),
         ],
         compiler_params=pltpu.CompilerParams(
             collective_id=0, has_side_effects=True, vmem_limit_bytes=56 * 2**20

time: 147 us -> 145 us (0.986)
    pallas_call x1, Pallas kernels: 144 us -> 143 us  [per_device(): pl.pallas_call(functools.partial(kernel, groups), out_shape=jax.ShapeDtyp...]
where the time goes in v3:
time: 145 us
  Pallas kernels  143 us (99%)
  local copies, waits for them, and re-layouts  2.26 us (2%)
    pallas_call x1, Pallas kernels, per_device(): pl.pallas_call(functools.partial(kernel, groups), out_shape=jax.ShapeDtyp...  143 us

profile of v3, /device:TPU:0, one launch (start us, length us, event | category | flops | bytes accessed | tf_op | source)
XLA Modules:
  0.0 144.8 jit_solution(9645039110057197825)
XLA Ops:
  0.0 142.5 %shard_map.73 = bf16[32,16384]{1,0:T(8,128)(2,1)} custom-call(bf16[32,16384]{1,0:T(8,128)(2,1)} %state.1, bf16[32,32768]{1,0:T(8,128)(2,1)} %predicted.1, bf16[32,32768]{1,0:T(8,128)(2,1)} %perturbed.1, f32[16,1,2048]{2,1,0:T(1,128)} %bitcast.2, s32[16,1,2048]{2,1,0:T(1,128)} %bitcast.3, s32[2,2]{1,0:T(2,128)} %row_count.1, s32[1,2,2048]{2,1,0:T(2,128)} %row_index.1), custom_call_target="tpu_custom_call" | custom-call | tf_op jit(solution)/shard_map/pallas_call | solution.py:299
  142.5 2.3 %copy.9 = bf16[32,16384]{1,0:T(8,128)(2,1)} copy(bf16[32,16384]{1,0:T(8,128)(2,1)} %shard_map.73) | data formatting | bytes 2097152
